TPU v7x, 32 devices: a whole 2x2x4 slice. The times are simulated.
32 devices in a mesh: ens: 2 (over y), row: 4 (over z), col: 4 (over x, core).
Axes of the slice: x: 2, y: 2, z: 4, core: 2. Of those that a mesh axis runs over, the one named last changes fastest.
Arguments:
- series: float32 [24576, 256], P(('ens', 'row', 'col')), parts along dimension 0, may hold values from -22 to 22, as said below
- vectors: float32 [24576, 128], P(('ens', 'row', 'col')), parts along dimension 0, may hold values from -6 to 6
- damp_class: int32 [24576], P(('ens', 'row', 'col')), parts along dimension 0, may hold values from 0 to 15
- damp_levels: float32 [16], replicated, may hold values from 0.5 to 2
- removed_blocks: int32 [64, 32], P('ens'), parts along dimension 0, may hold values 0 or 1
Outputs:
- filtered: float32 [24576, 128], P(('ens', 'row', 'col')), parts along dimension 0
There are 2 independent parts, one for each index of `ens`. A program takes and returns all parts, laid end to end along the dimension named above; an argument that names none is the same for every part. Nothing has to cross between parts.
Inputs may be any that keep to these rules, and one draw needn't show every extreme that they name: Each voxel's series is not constant.
All inputs are finite; a program needn't handle non-finite values.
Results may differ from a plain program's by a relative error of at most 0.0003.
Values sent between devices are 32-bit elements; how exact they have to be, the bound alone decides.
No kernel may reach another device: no remote copies, remote signals or barrier semaphores. Data moves between devices by JAX's collectives and lax.ppermute only.
A program may use at most 128 MiB of HBM per device.

v0:
```python
import jax
import jax.numpy as jnp
from jax import lax
from jax.sharding import PartitionSpec as P

N = 12288
sharpness = 12.0


def standardize(series):
    centered = series - jnp.mean(series, axis=1, keepdims=True)
    spread = jnp.mean(centered * centered, axis=1, keepdims=True)
    return centered * lax.rsqrt(spread + 1e-05)


def local(series, vectors, damp_class, damp_levels, removed_blocks):
    n_col = lax.axis_size("col")
    row_id = lax.axis_index("row")
    col_id = lax.axis_index("col")
    shard_rows = series.shape[0]
    samples = series.shape[1]
    classes = damp_levels.shape[0]
    z_own = standardize(series)
    onehot = (damp_class[:, None] == jnp.arange(classes, dtype=jnp.int32)[None, :]).astype(
        jnp.float32
    )
    damping = jnp.sum(onehot * damp_levels[None, :], axis=1)
    z_rows, d_rows = (
        lax.all_gather(z_own, "col", axis=0, tiled=True),
        lax.all_gather(damping, "col", axis=0, tiled=True),
    )
    tile_rows = z_rows.shape[0]
    blocks = removed_blocks.shape[0]
    block_size = N // blocks
    row_blocks = tile_rows // block_size
    keep_rows = 1.0 - lax.dynamic_slice_in_dim(
        removed_blocks, row_id * row_blocks, row_blocks, 0
    ).astype(jnp.float32)
    shard_piece = lax.all_gather(z_own, "row", axis=0, tiled=True)
    count = shard_piece.shape[0]
    position = jnp.arange(count, dtype=jnp.int32)
    owner_row = position // shard_rows
    global_index = (owner_row * n_col + col_id) * shard_rows + position % shard_rows
    col_block = global_index // block_size
    onehot_cols = (col_block[None, :] == jnp.arange(blocks, dtype=jnp.int32)[:, None]).astype(
        jnp.float32
    )
    keep_small = jnp.dot(
        keep_rows, onehot_cols, precision=lax.Precision.HIGHEST, preferred_element_type=jnp.float32
    )
    keep_full = jnp.broadcast_to(keep_small[:, None, :], (row_blocks, block_size, count)).reshape(
        tile_rows, count
    )
    correlation = (
        lax.dot_general(
            z_rows,
            shard_piece,
            (((1,), (1,)), ((), ())),
            precision=lax.Precision.HIGHEST,
            preferred_element_type=jnp.float32,
        )
        / samples
    )
    affinity = jnp.tanh(sharpness * correlation) * keep_full * d_rows[:, None]
    spectral_scale = 0.5 * N * jnp.mean(damp_levels * damp_levels)

    def forward_add(shard_piece):
        return jnp.dot(
            affinity,
            shard_piece,
            precision=lax.Precision.HIGHEST,
            preferred_element_type=jnp.float32,
        )

    def backward_add(shard_piece):
        return lax.dot_general(
            affinity,
            shard_piece,
            (((0,), (0,)), ((), ())),
            precision=lax.Precision.HIGHEST,
            preferred_element_type=jnp.float32,
        )

    def normal_apply(field_in):
        product = forward_add(lax.all_gather(field_in, "row", axis=0, tiled=True))
        product = lax.psum_scatter(product, "col", scatter_dimension=0, tiled=True)
        returned = backward_add(lax.all_gather(product, "col", axis=0, tiled=True))
        return lax.psum_scatter(returned, "row", scatter_dimension=0, tiled=True) / spectral_scale

    first_term = normal_apply(vectors) - vectors
    filtered = 2.0 * (normal_apply(first_term) - first_term) - vectors
    return filtered


def solution(mesh):
    placed = (
        P(("ens", "row", "col"), None),
        P(("ens", "row", "col"), None),
        P(("ens", "row", "col")),
        P(),
        P("ens", None),
    )
    return jax.shard_map(
        local, mesh=mesh, in_specs=placed, out_specs=P(("ens", "row", "col"), None), check_vma=False
    )
```

profile of v0, /device:TPU:0, one launch (start us, length us, event | category | flops | bytes accessed | tf_op | source)
XLA Modules:
  0.0 560.3 jit_solution(4432875654553335063)
XLA Ops:
  6.5 1.3 reduce_sum.36
  7.9 1.4 multiply_reduce_fusion
  9.3 2.3 subtract_multiply_fusion
  11.6 0.0 all-gather.8.cloned.1.call-start
  11.7 0.7 all-gather.8.cloned.1.call-update
  12.4 0.7 all-gather.12.cloned.1.call-update
  13.1 0.0 reduce-scatter.5.cloned.1.call-start
  13.2 0.1 select_reduce_fusion
  13.3 6.2 %all-gather = f32[4,1,768]{2,1,0:T(1,128)S(1)} all-gather(f32[1,1,768]{2,1,0:T(1,128)S(1)} %reshape.49), channel_id=1, replica_groups=mesh['ens'=2,'row'=4,'col'=4] {'col'}, dimensions={0}, use_global_device_ids=true | all-gather | bytes 15360 | tf_op jit(solution)/shard_map/all_gather | solution.py:30
  19.5 0.9 fusion.1
  20.5 57.5 %all-gather.10.cloned.1.call-done = f32[3072,256]{1,0:T(8,128)} async-done(((f32[768,256]{1,0:T(8,128)}), f32[3072,256]{1,0:T(8,128)}) %all-gather.10.cloned.1.call-update) | async-done | bytes 3145744 | tf_op jit(solution)/shard_map/all_gather | solution.py:39
  78.0 28.7 %all-gather.8.cloned.1.call-done = f32[3072,256]{1,0:T(8,128)} async-done(((f32[768,256]{1,0:T(8,128)}), f32[3072,256]{1,0:T(8,128)}) %all-gather.8.cloned.1.call-update) | async-done | bytes 3145744 | tf_op jit(solution)/shard_map/all_gather | solution.py:29
  106.7 40.0 %fusion = f32[3072,3072]{1,0:T(8,128)} fusion(f32[3072,256]{1,0:T(8,128)} %all-gather.8.cloned.1.call-done, f32[3072,256]{1,0:T(8,128)} %all-gather.10.cloned.1.call-done, f32[3072]{0:T(1024)S(1)} %bitcast.15, f32[8,3072]{1,0:T(8,128)S(1)} %fusion.1), kind=kOutput, calls=%fused_computation.1 | convolution fusion | flops 29019340800 | bytes 44150784 | tf_op jit(solution)/shard_map/dot_general | solution.py:55
  146.7 34.9 %fusion.21 = f32[3072,128]{1,0:T(8,128)} fusion(f32[3072,3072]{1,0:T(8,128)} %fusion, f32[3072,128]{1,0:T(8,128)} %all-gather.12.cloned.1.call-done), kind=kOutput, calls=%fused_computation.39 | convolution fusion | flops 14495514624 | bytes 40894464 | tf_op jit(solution)/shard_map/dot_general | solution.py:68
  181.6 0.0 all-gather.14.cloned.1.call-start
  181.7 28.1 %reduce-scatter.5.cloned.1.call-done = f32[768,128]{1,0:T(8,128)} async-done(((f32[3072,128]{1,0:T(8,128)}), f32[768,128]{1,0:T(8,128)}) %reduce-scatter.5.cloned.1.call-update) | async-done | bytes 393232 | tf_op jit(solution)/shard_map/reduce_scatter | solution.py:86
  209.8 0.0 reduce-scatter.7.cloned.1.call-start
  209.9 21.0 %all-gather.14.cloned.1.call-done = f32[3072,128]{1,0:T(8,128)} async-done(((f32[768,128]{1,0:T(8,128)}), f32[3072,128]{1,0:T(8,128)}) %all-gather.14.cloned.1.call-update) | async-done | bytes 1572880 | tf_op jit(solution)/shard_map/all_gather | solution.py:87
  230.9 64.5 %fusion.22 = f32[3072,128]{1,0:T(8,128)} fusion(f32[3072,3072]{1,0:T(8,128)} %fusion, f32[3072,128]{1,0:T(8,128)} %all-gather.14.cloned.1.call-done), kind=kOutput, calls=%fused_computation.40 | convolution fusion | flops 14495514624 | bytes 40894464 | tf_op jit(solution)/shard_map/dot_general | solution.py:76
  295.4 0.0 all-gather.16.cloned.1.call-start
  295.5 0.6 multiply_reduce_fusion.1
  296.7 34.3 %reduce-scatter.7.cloned.1.call-done = f32[768,128]{1,0:T(8,128)} async-done(((f32[3072,128]{1,0:T(8,128)}), f32[768,128]{1,0:T(8,128)}) %reduce-scatter.7.cloned.1.call-update) | async-done | bytes 393232 | tf_op jit(solution)/shard_map/reduce_scatter | solution.py:88
  331.0 1.8 divide_subtract_fusion
  332.8 0.0 reduce-scatter.9.cloned.1.call-start
  332.9 36.0 %all-gather.16.cloned.1.call-done = f32[3072,128]{1,0:T(8,128)} async-done(((f32[768,128]{1,0:T(8,128)}), f32[3072,128]{1,0:T(8,128)}) %all-gather.16.cloned.1.call-update) | async-done | bytes 1572880 | tf_op jit(solution)/shard_map/all_gather | solution.py:85
  368.8 34.7 %fusion.23 = f32[3072,128]{1,0:T(8,128)} fusion(f32[3072,3072]{1,0:T(8,128)} %fusion, f32[3072,128]{1,0:T(8,128)} %all-gather.16.cloned.1.call-done), kind=kOutput, calls=%fused_computation.41 | convolution fusion | flops 14495514624 | bytes 40894464 | tf_op jit(solution)/shard_map/dot_general | solution.py:68
  403.6 0.0 all-gather.18.cloned.1.call-start
  403.6 27.0 %reduce-scatter.9.cloned.1.call-done = f32[768,128]{1,0:T(8,128)} async-done(((f32[3072,128]{1,0:T(8,128)}), f32[768,128]{1,0:T(8,128)}) %reduce-scatter.9.cloned.1.call-update) | async-done | bytes 393232 | tf_op jit(solution)/shard_map/reduce_scatter | solution.py:86
  430.7 21.1 %all-gather.18.cloned.1.call-done = f32[3072,128]{1,0:T(8,128)} async-done(((f32[768,128]{1,0:T(8,128)}), f32[3072,128]{1,0:T(8,128)}) %all-gather.18.cloned.1.call-update) | async-done | bytes 1572880 | tf_op jit(solution)/shard_map/all_gather | solution.py:87
  451.8 64.0 %fusion.24 = f32[3072,128]{1,0:T(8,128)} fusion(f32[3072,3072]{1,0:T(8,128)} %fusion, f32[3072,128]{1,0:T(8,128)} %all-gather.18.cloned.1.call-done), kind=kOutput, calls=%fused_computation.42 | convolution fusion | flops 14495514624 | bytes 40894464 | tf_op jit(solution)/shard_map/dot_general | solution.py:76
  515.9 35.6 %reduce-scatter.11.cloned.1.call-done = f32[768,128]{1,0:T(8,128)} async-done(((f32[3072,128]{1,0:T(8,128)}), f32[768,128]{1,0:T(8,128)}) %reduce-scatter.11.cloned.1.call-update) | async-done | bytes 393232 | tf_op jit(solution)/shard_map/reduce_scatter | solution.py:88
  551.5 1.8 multiply_subtract_fusion
  (24 shorter events, 0.3 us)
Async XLA Ops:
  6.5 6.6 %copy-start.2 = (s32[768]{0:T(1024)S(1)}, s32[768]{0:T(1024)}, u32[]{:S(2)}) copy-start(s32[768]{0:T(1024)} %param.7) | copy-start | bytes 9220
  6.5 6.7 %copy-start.3 = (f32[16]{0:T(128)S(1)}, f32[16]{0:T(128)}, u32[]{:S(2)}) copy-start(f32[16]{0:T(128)} %param.8) | copy-start | bytes 196
  6.5 71.4 %all-gather.10.cloned.1.call-start = ((), (), s32[]{:S(2)}) async-start(), calls=%async_computation.5 | async-start | bytes 3932160 | tf_op jit(solution)/shard_map/all_gather | solution.py:39
  11.6 95.1 %all-gather.8.cloned.1.call-start = ((), (), s32[]{:S(2)}) async-start(), calls=%async_computation.4 | async-start | bytes 3932160 | tf_op jit(solution)/shard_map/all_gather | solution.py:29
  12.4 134.3 %all-gather.12.cloned.1.call-start = ((), (), s32[]{:S(2)}) async-start(), calls=%async_computation.6 | async-start | bytes 1966080 | tf_op jit(solution)/shard_map/all_gather | solution.py:85
  13.1 196.7 %reduce-scatter.5.cloned.1.call-start = ((), (), s32[]{:S(2)}) async-start(), calls=%async_computation.7 | async-start | bytes 1966080 | tf_op jit(solution)/shard_map/reduce_scatter | solution.py:86
  181.6 49.3 %all-gather.14.cloned.1.call-start = ((), (), s32[]{:S(2)}) async-start(), calls=%async_computation.8 | async-start | bytes 1966080 | tf_op jit(solution)/shard_map/all_gather | solution.py:87
  209.8 121.2 %copy-start = (f32[768,128]{1,0:T(8,128)S(1)}, f32[768,128]{1,0:T(8,128)}, u32[]{:S(2)}) copy-start(f32[768,128]{1,0:T(8,128)} %param.6) | copy-start | bytes 1179652
  209.8 121.2 %reduce-scatter.7.cloned.1.call-start = ((), (), s32[]{:S(2)}) async-start(), calls=%async_computation.9 | async-start | bytes 1966080 | tf_op jit(solution)/shard_map/reduce_scatter | solution.py:88
  295.4 73.4 %all-gather.16.cloned.1.call-start = ((), (), s32[]{:S(2)}) async-start(), calls=%async_computation.10 | async-start | bytes 1966080 | tf_op jit(solution)/shard_map/all_gather | solution.py:85
  332.8 97.8 %reduce-scatter.9.cloned.1.call-start = ((), (), s32[]{:S(2)}) async-start(), calls=%async_computation.11 | async-start | bytes 1966080 | tf_op jit(solution)/shard_map/reduce_scatter | solution.py:86
  403.6 48.2 %all-gather.18.cloned.1.call-start = ((), (), s32[]{:S(2)}) async-start(), calls=%async_computation.12 | async-start | bytes 1966080 | tf_op jit(solution)/shard_map/all_gather | solution.py:87
  430.6 120.8 %copy-start.1 = (f32[768,128]{1,0:T(8,128)S(1)}, f32[768,128]{1,0:T(8,128)}, u32[]{:S(2)}) copy-start(f32[768,128]{1,0:T(8,128)} %reduce-scatter.7.cloned.1.call-done) | copy-start | bytes 1179652
  430.6 120.8 %reduce-scatter.11.cloned.1.call-start = ((), (), s32[]{:S(2)}) async-start(), calls=%async_computation.13 | async-start | bytes 1966080 | tf_op jit(solution)/shard_map/reduce_scatter | solution.py:88
Sparse Core Ops, SparseCore 0:
  11.8 66.1 all-gather.9
  79.5 27.1 all-gather.7
  108.3 37.0 all-gather.11
  181.7 28.0 reduce-scatter.4
  211.2 19.6 all-gather.13
  295.5 35.4 reduce-scatter.6
  332.9 35.8 all-gather.15
  403.7 26.8 reduce-scatter.8
  432.2 19.6 all-gather.17
  516.0 35.4 reduce-scatter.10
where the time goes:
time: 568 us; the launch traced here: 560 us
  waiting for transfers between devices  291 us (51%)
  matrix products  239 us (42%)
  between operations  14.5 us (3%)
  other arithmetic  9.36 us (2%)
  blocking collectives  6.21 us (1%)
    dot_general x2, matrix products, backward_add(): lax.dot_general(affinity, shard_piece, (((0,), (0,)), ((), ())), precisio...  129 us
    reduce_scatter x2, waiting for transfers between devices, normal_apply(): lax.psum_scatter(returned, 'row', scatter_dimension=0, tiled=True)  69.9 us
    dot_general x2, matrix products, forward_add(): jnp.dot(affinity, shard_piece, precision=lax.Precision.HIGHEST, preferred...  69.6 us
    all_gather x1, waiting for transfers between devices, local(): shard_piece = lax.all_gather(z_own, 'row', axis=0, tiled=True)  57.5 us
    reduce_scatter x2, waiting for transfers between devices, normal_apply(): product = lax.psum_scatter(product, 'col', scatter_dimension=0, tiled=True)  55.1 us
    all_gather x2, waiting for transfers between devices, normal_apply(): returned = backward_add(lax.all_gather(product, 'col', axis=0, tiled=True))  42.1 us
    dot_general x1, matrix products, local(): lax.dot_general(z_rows, shard_piece, (((1,), (1,)), ((), ())), precision=...  40 us
    all_gather x2, waiting for transfers between devices, normal_apply(): product = forward_add(lax.all_gather(field_in, 'row', axis=0, tiled=True))  36 us
  transfers between devices with their start and end apart: 10, of which 9 were waited for; matrix products, arithmetic and copies ran while one was open for 7% of the time, Pallas kernels for 0%

commit v1 on v0

--- a/solution.py
+++ b/solution.py
@@ -36,7 +36,12 @@
     keep_rows = 1.0 - lax.dynamic_slice_in_dim(
         removed_blocks, row_id * row_blocks, row_blocks, 0
     ).astype(jnp.float32)
-    shard_piece = lax.all_gather(z_own, "row", axis=0, tiled=True)
+    ring = [z_own]
+    for hop in range(3):
+        ring.append(lax.ppermute(ring[-1], "row", [(dev, (dev + 1) % 4) for dev in range(4)]))
+    shard_piece = jnp.roll(
+        jnp.concatenate(ring[::-1], axis=0), (lax.axis_index("row") + 1) * ring[0].shape[0], axis=0
+    )
     count = shard_piece.shape[0]
     position = jnp.arange(count, dtype=jnp.int32)
     owner_row = position // shard_rows

time: 568 us -> 547 us (0.963)
  waiting for transfers between devices: 291 us -> 265 us
    ppermute x0 -> x3, waiting for transfers between devices: none -> 61.6 us  [local(): lax.ppermute(ring[-1], 'row', [(dev, (dev + 1) % 4) for dev in range(4)])]
    all_gather x1 -> x0, waiting for transfers between devices: 57.5 us -> none  [local(): shard_piece = lax.all_gather(z_own, 'row', axis=0, tiled=True)]
    all_gather x1, waiting for transfers between devices: 28.7 us -> 0.02 us  [local(): lax.all_gather(z_own, 'col', axis=0, tiled=True)]
  transfers between devices with their start and end apart: 10 -> 12, of which waited for: 9 -> 10; matrix products, arithmetic and copies ran while one was open for 7% -> 8% of each run, Pallas kernels for 0% -> 0%
where the time goes in v1:
time: 547 us; the launch traced here: 538 us
  waiting for transfers between devices  265 us (48%)
  matrix products  239 us (44%)
  between operations  14.3 us (3%)
  other arithmetic  10.7 us (2%)
    dot_general x2, matrix products, backward_add(): lax.dot_general(affinity, shard_piece, (((0,), (0,)), ((), ())), precisio...  129 us
    reduce_scatter x2, waiting for transfers between devices, normal_apply(): lax.psum_scatter(returned, 'row', scatter_dimension=0, tiled=True)  69.9 us
    dot_general x2, matrix products, forward_add(): jnp.dot(affinity, shard_piece, precision=lax.Precision.HIGHEST, preferred...  69.6 us
    ppermute x3, waiting for transfers between devices, local(): lax.ppermute(ring[-1], 'row', [(dev, (dev + 1) % 4) for dev in range(4)])  61.6 us
    reduce_scatter x2, waiting for transfers between devices, normal_apply(): product = lax.psum_scatter(product, 'col', scatter_dimension=0, tiled=True)  55.5 us
    all_gather x2, waiting for transfers between devices, normal_apply(): returned = backward_add(lax.all_gather(product, 'col', axis=0, tiled=True))  42.2 us
    dot_general x1, matrix products, local(): lax.dot_general(z_rows, shard_piece, (((1,), (1,)), ((), ())), precision=...  39.9 us
    all_gather x2, waiting for transfers between devices, normal_apply(): product = forward_add(lax.all_gather(field_in, 'row', axis=0, tiled=True))  36 us
  transfers between devices with their start and end apart: 12, of which 10 were waited for; matrix products, arithmetic and copies ran while one was open for 8% of the time, Pallas kernels for 0%

profile of v1, /device:TPU:0, one launch (start us, length us, event | category | flops | bytes accessed | tf_op | source)
XLA Modules:
  0.0 538.2 jit_solution(14721913795259209321)
XLA Ops:
  6.5 1.4 reduce_sum.36
  7.9 1.4 multiply_reduce_fusion
  9.4 2.3 subtract_multiply_fusion
  11.7 3.1 collective-permute-start
  14.8 19.8 %collective-permute-done = f32[768,256]{1,0:T(8,128)S(1)} collective-permute-done((f32[768,256]{1,0:T(8,128)}, f32[768,256]{1,0:T(8,128)S(1)}, u32[]{:S(2)}, u32[]{:S(2)}) %collective-permute-start) | collective-permute-done | bytes 786464 | tf_op jit(solution)/shard_map/ppermute | solution.py:41
  34.6 20.5 %collective-permute-done.1 = f32[768,256]{1,0:T(8,128)S(1)} collective-permute-done((f32[768,256]{1,0:T(8,128)S(1)}, f32[768,256]{1,0:T(8,128)S(1)}, u32[]{:S(2)}, u32[]{:S(2)}) %collective-permute-start.1) | collective-permute-done | bytes 786464 | tf_op jit(solution)/shard_map/ppermute | solution.py:41
  55.2 0.8 select_reduce_fusion
  56.0 5.2 all-gather
  61.2 0.9 fusion.2
  62.2 21.3 %collective-permute-done.2 = f32[768,256]{1,0:T(8,128)S(1)} collective-permute-done((f32[768,256]{1,0:T(8,128)S(1)}, f32[768,256]{1,0:T(8,128)S(1)}, u32[]{:S(2)}, u32[]{:S(2)}) %collective-permute-start.2) | collective-permute-done | bytes 786464 | tf_op jit(solution)/shard_map/ppermute | solution.py:41
  83.5 0.1 constant_dynamic-update-slice_fusion.6
  83.6 0.1 constant_dynamic-update-slice_fusion.5
  83.6 0.3 constant_dynamic-update-slice_fusion.4
  83.9 0.1 constant_dynamic-update-slice_fusion.3
  84.0 0.1 constant_dynamic-update-slice_fusion.2
  84.1 0.3 constant_dynamic-update-slice_fusion
  84.4 0.3 fusion.39
  84.7 39.9 %fusion = f32[3072,3072]{1,0:T(8,128)} fusion(f32[3072,256]{1,0:T(8,128)} %all-gather.7.cloned.1.call-done, f32[3072]{0:T(1024)S(1)} %bitcast.17, f32[8,3072]{1,0:T(8,128)S(1)} %fusion.2, f32[3072,256]{1,0:T(8,128)S(1)} %fusion.39), kind=kOutput, calls=%fused_computation.1 | convolution fusion | flops 29019340800 | bytes 44150784 | tf_op jit(solution)/shard_map/dot_general | solution.py:60
  124.5 34.9 %fusion.23 = f32[3072,128]{1,0:T(8,128)} fusion(f32[3072,3072]{1,0:T(8,128)} %fusion, f32[3072,128]{1,0:T(8,128)} %all-gather.9.cloned.1.call-done), kind=kOutput, calls=%fused_computation.49 | convolution fusion | flops 14495514624 | bytes 40894464 | tf_op jit(solution)/shard_map/dot_general | solution.py:73
  159.5 28.5 %reduce-scatter.5.cloned.1.call-done = f32[768,128]{1,0:T(8,128)} async-done(((f32[3072,128]{1,0:T(8,128)}), f32[768,128]{1,0:T(8,128)}) %reduce-scatter.5.cloned.1.call-update) | async-done | bytes 393232 | tf_op jit(solution)/shard_map/reduce_scatter | solution.py:91
  188.1 21.0 %all-gather.11.cloned.1.call-done = f32[3072,128]{1,0:T(8,128)} async-done(((f32[768,128]{1,0:T(8,128)}), f32[3072,128]{1,0:T(8,128)}) %all-gather.11.cloned.1.call-update) | async-done | bytes 1572880 | tf_op jit(solution)/shard_map/all_gather | solution.py:92
  209.1 64.5 %fusion.24 = f32[3072,128]{1,0:T(8,128)} fusion(f32[3072,3072]{1,0:T(8,128)} %fusion, f32[3072,128]{1,0:T(8,128)} %all-gather.11.cloned.1.call-done), kind=kOutput, calls=%fused_computation.50 | convolution fusion | flops 14495514624 | bytes 40894464 | tf_op jit(solution)/shard_map/dot_general | solution.py:81
  273.7 0.6 multiply_reduce_fusion.1
  274.9 34.3 %reduce-scatter.7.cloned.1.call-done = f32[768,128]{1,0:T(8,128)} async-done(((f32[3072,128]{1,0:T(8,128)}), f32[768,128]{1,0:T(8,128)}) %reduce-scatter.7.cloned.1.call-update) | async-done | bytes 393232 | tf_op jit(solution)/shard_map/reduce_scatter | solution.py:93
  309.2 1.8 divide_subtract_fusion
  311.0 36.0 %all-gather.13.cloned.1.call-done = f32[3072,128]{1,0:T(8,128)} async-done(((f32[768,128]{1,0:T(8,128)}), f32[3072,128]{1,0:T(8,128)}) %all-gather.13.cloned.1.call-update) | async-done | bytes 1572880 | tf_op jit(solution)/shard_map/all_gather | solution.py:90
  347.0 34.7 %fusion.25 = f32[3072,128]{1,0:T(8,128)} fusion(f32[3072,3072]{1,0:T(8,128)} %fusion, f32[3072,128]{1,0:T(8,128)} %all-gather.13.cloned.1.call-done), kind=kOutput, calls=%fused_computation.51 | convolution fusion | flops 14495514624 | bytes 40894464 | tf_op jit(solution)/shard_map/dot_general | solution.py:73
  381.8 27.0 %reduce-scatter.9.cloned.1.call-done = f32[768,128]{1,0:T(8,128)} async-done(((f32[3072,128]{1,0:T(8,128)}), f32[768,128]{1,0:T(8,128)}) %reduce-scatter.9.cloned.1.call-update) | async-done | bytes 393232 | tf_op jit(solution)/shard_map/reduce_scatter | solution.py:91
  408.9 21.2 %all-gather.15.cloned.1.call-done = f32[3072,128]{1,0:T(8,128)} async-done(((f32[768,128]{1,0:T(8,128)}), f32[3072,128]{1,0:T(8,128)}) %all-gather.15.cloned.1.call-update) | async-done | bytes 1572880 | tf_op jit(solution)/shard_map/all_gather | solution.py:92
  430.1 64.0 %fusion.26 = f32[3072,128]{1,0:T(8,128)} fusion(f32[3072,3072]{1,0:T(8,128)} %fusion, f32[3072,128]{1,0:T(8,128)} %all-gather.15.cloned.1.call-done), kind=kOutput, calls=%fused_computation.52 | convolution fusion | flops 14495514624 | bytes 40894464 | tf_op jit(solution)/shard_map/dot_general | solution.py:81
  494.1 35.6 %reduce-scatter.11.cloned.1.call-done = f32[768,128]{1,0:T(8,128)} async-done(((f32[3072,128]{1,0:T(8,128)}), f32[768,128]{1,0:T(8,128)}) %reduce-scatter.11.cloned.1.call-update) | async-done | bytes 393232 | tf_op jit(solution)/shard_map/reduce_scatter | solution.py:93
  529.7 1.8 multiply_subtract_fusion
  (36 shorter events, 0.7 us)
Async XLA Ops:
  6.5 77.1 %copy-start = (f32[768,256]{1,0:T(8,128)S(1)}, f32[768,256]{1,0:T(8,128)}, u32[]{:S(2)}) copy-start(f32[768,256]{1,0:T(8,128)} %param.5) | copy-start | bytes 2359300
  6.5 78.1 %all-gather.7.cloned.1.call-start = ((), (), s32[]{:S(2)}) async-start(), calls=%async_computation.4 | async-start | bytes 3932160 | tf_op jit(solution)/shard_map/all_gather | solution.py:29
  11.7 112.8 %all-gather.9.cloned.1.call-start = ((), (), s32[]{:S(2)}) async-start(), calls=%async_computation.5 | async-start | bytes 1966080 | tf_op jit(solution)/shard_map/all_gather | solution.py:90
  11.7 22.9 %collective-permute-start = (f32[768,256]{1,0:T(8,128)}, f32[768,256]{1,0:T(8,128)S(1)}, u32[]{:S(2)}, u32[]{:S(2)}) collective-permute-start(f32[768,256]{1,0:T(8,128)} %subtract_multiply_fusion), channel_id=1, source_target_pairs={{0,4},{4,8},{8,12},{12,0},{1,5},{5,9},{9,13},{13,1},{2,6},{6,10},{... | collective-permute-start | bytes 2359304 | tf_op jit(solution)/shard_map/ppermute | solution.py:41
  34.6 20.5 %collective-permute-start.1 = (f32[768,256]{1,0:T(8,128)S(1)}, f32[768,256]{1,0:T(8,128)S(1)}, u32[]{:S(2)}, u32[]{:S(2)}) collective-permute-start(f32[768,256]{1,0:T(8,128)S(1)} %collective-permute-done), channel_id=1, source_target_pairs={{0,4},{4,8},{8,12},{12,0},{1,5},{5,9},{9,13},{13,1},{2,6},{6,10},{... | collective-permute-start | bytes 2359304 | tf_op jit(solution)/shard_map/ppermute | solution.py:41
  55.1 28.3 %collective-permute-start.2 = (f32[768,256]{1,0:T(8,128)S(1)}, f32[768,256]{1,0:T(8,128)S(1)}, u32[]{:S(2)}, u32[]{:S(2)}) collective-permute-start(f32[768,256]{1,0:T(8,128)S(1)} %collective-permute-done.1), channel_id=1, source_target_pairs={{0,4},{4,8},{8,12},{12,0},{1,5},{5,9},{9,13},{13,1},{2,6},{6,10},{... | collective-permute-start | bytes 2359304 | tf_op jit(solution)/shard_map/ppermute | solution.py:41
  55.1 132.8 %reduce-scatter.5.cloned.1.call-start = ((), (), s32[]{:S(2)}) async-start(), calls=%async_computation.6 | async-start | bytes 1966080 | tf_op jit(solution)/shard_map/reduce_scatter | solution.py:91
  159.4 49.6 %all-gather.11.cloned.1.call-start = ((), (), s32[]{:S(2)}) async-start(), calls=%async_computation.7 | async-start | bytes 1966080 | tf_op jit(solution)/shard_map/all_gather | solution.py:92
  188.0 85.7 %copy-start.3 = (f32[16]{0:T(128)S(1)}, f32[16]{0:T(128)}, u32[]{:S(2)}) copy-start(f32[16]{0:T(128)} %param.8) | copy-start | bytes 196
  188.0 121.2 %copy-start.1 = (f32[768,128]{1,0:T(8,128)S(1)}, f32[768,128]{1,0:T(8,128)}, u32[]{:S(2)}) copy-start(f32[768,128]{1,0:T(8,128)} %param.6) | copy-start | bytes 1179652
  188.0 121.2 %reduce-scatter.7.cloned.1.call-start = ((), (), s32[]{:S(2)}) async-start(), calls=%async_computation.8 | async-start | bytes 1966080 | tf_op jit(solution)/shard_map/reduce_scatter | solution.py:93
  273.6 73.4 %all-gather.13.cloned.1.call-start = ((), (), s32[]{:S(2)}) async-start(), calls=%async_computation.9 | async-start | bytes 1966080 | tf_op jit(solution)/shard_map/all_gather | solution.py:90
  311.0 97.8 %reduce-scatter.9.cloned.1.call-start = ((), (), s32[]{:S(2)}) async-start(), calls=%async_computation.10 | async-start | bytes 1966080 | tf_op jit(solution)/shard_map/reduce_scatter | solution.py:91
  381.8 48.3 %all-gather.15.cloned.1.call-start = ((), (), s32[]{:S(2)}) async-start(), calls=%async_computation.11 | async-start | bytes 1966080 | tf_op jit(solution)/shard_map/all_gather | solution.py:92
  408.9 120.8 %copy-start.2 = (f32[768,128]{1,0:T(8,128)S(1)}, f32[768,128]{1,0:T(8,128)}, u32[]{:S(2)}) copy-start(f32[768,128]{1,0:T(8,128)} %reduce-scatter.7.cloned.1.call-done) | copy-start | bytes 1179652
  408.9 120.8 %reduce-scatter.11.cloned.1.call-start = ((), (), s32[]{:S(2)}) async-start(), calls=%async_computation.12 | async-start | bytes 1966080 | tf_op jit(solution)/shard_map/reduce_scatter | solution.py:93
Sparse Core Ops, SparseCore 0:
  11.8 31.2 all-gather.6
  55.3 45.2 all-gather.8
  159.6 28.3 reduce-scatter.4
  189.4 19.6 all-gather.10
  273.7 35.4 reduce-scatter.6
  311.1 35.8 all-gather.12
  381.9 26.8 reduce-scatter.8
  410.4 19.6 all-gather.14
  494.2 35.4 reduce-scatter.10
